TPU v7x, 32 devices: a whole 2x2x4 slice. The times are simulated.
32 devices in a mesh: doc: 4 (over z), feat: 8 (over y, x, core).
Axes of the slice: x: 2, y: 2, z: 4, core: 2. Of those that a mesh axis runs over, the one named last changes fastest.
Arguments:
- documents: bfloat16 [512, 512], P('doc', 'feat'), may hold values from -6 to 6
- directions: bfloat16 [512, 32768], P('doc', 'feat'), may hold values from -0.5 to 0.5
- phase: float32 [32768], P('feat'), may hold values from -3.140625 to 3.140625
- amplitude: float32 [32768], P('feat'), may hold values from 0.4 to 2.3
- doc_weight: float32 [512], P('doc'), may hold values from 0.5 to 4.2
- labels: int32 [512], P('doc'), may hold values from 0 to 127
Outputs:
- margins: float32 [512, 128], P('doc')
- scaled_weights: float32 [32768, 128], P('feat')
All inputs are finite; a program needn't handle non-finite values.
Results may differ from a plain program's by a relative error of at most 0.0003.
Values may be sent and summed in bfloat16 or wider, within the bound.
A program may use at most 64 MiB of HBM per device.

v0:
```python
import jax
import jax.numpy as jnp
from jax import lax
from jax.sharding import PartitionSpec as P

C = 128
ITERS = 3
NEWTON = 3
HI = lax.Precision.HIGHEST
shrink_level = 0.1
ratio_floor = 1e-06


def logistic_prox(target, signs, weight_ratio):
    current = target
    for newton_step in range(NEWTON):
        chance = jax.nn.sigmoid(-signs * current)
        gradient = current - target - weight_ratio * signs * chance
        current = current - gradient / (1.0 + weight_ratio * chance * (1.0 - chance))
    return current


def shrink_values(target, limit):
    return target - jnp.clip(target, -limit, limit)


def per_device(documents, directions, phase, amplitude, doc_weight, labels):
    doc_count = documents.shape[0]
    width_tile = directions.shape[1]
    num_feat = lax.axis_size("feat")
    num_doc = lax.axis_size("doc")
    chunk = width_tile // num_doc
    row = lax.axis_index("doc")
    doc_rows = lax.all_gather(documents, "feat", axis=1, tiled=True)
    doc_full = lax.all_gather(doc_rows, "doc", axis=0, tiled=True)
    dir_chunk = lax.all_to_all(directions, "doc", split_axis=1, concat_axis=0, tiled=True)
    phase_c = lax.dynamic_slice_in_dim(phase, row * chunk, chunk, 0)
    amp_c = lax.dynamic_slice_in_dim(amplitude, row * chunk, chunk, 0)
    angles = jnp.dot(doc_full, dir_chunk, preferred_element_type=jnp.float32)
    features = jnp.sqrt(2.0 / width_tile) * amp_c * jnp.cos(angles + phase_c)
    blocks = features.reshape(num_doc, doc_count, chunk)
    gram = jnp.einsum("iac,ibc->iab", blocks, blocks, precision=HI)
    gram = lax.psum_scatter(gram, "doc", scatter_dimension=0, tiled=True)[0]
    eye = jnp.eye(doc_count, dtype=jnp.float32)
    factor = jnp.linalg.cholesky(eye + gram)
    lower_inv = lax.linalg.triangular_solve(factor, eye, left_side=True, lower=True)
    inverse = lax.dot_general(lower_inv, lower_inv, (((0,), (0,)), ((), ())), precision=HI)
    signs = jnp.where(labels[:, None] == jnp.arange(C, dtype=jnp.int32)[None, :], 1.0, -1.0).astype(
        jnp.float32
    )
    share_rows = doc_count // num_feat
    offset = lax.axis_index("feat") * share_rows
    signs = lax.dynamic_slice_in_dim(signs, offset, share_rows, 0)
    weight = lax.dynamic_slice_in_dim(doc_weight, offset, share_rows, 0)[:, None]
    rho = jnp.float32(1.0)
    margins = logistic_prox(jnp.zeros(signs.shape, jnp.float32), signs, weight / rho)
    sums = jnp.zeros(signs.shape, jnp.float32)
    duals_y = jnp.zeros(signs.shape, jnp.float32)
    part = jnp.zeros((doc_count, C), jnp.float32)
    image = jnp.zeros((doc_count, C), jnp.float32)
    weights = jnp.zeros((chunk, C), jnp.float32)
    product = jnp.zeros((doc_count, C), jnp.float32)
    for step in range(ITERS):
        correction = (margins - duals_y - sums) / num_feat
        correction = lax.all_gather(correction, "feat", axis=0, tiled=True)
        target = part + correction
        residue = target - image
        solved = jnp.dot(inverse, residue, precision=HI)
        applied = residue - solved
        part = target - solved
        sums = lax.psum_scatter(part, "feat", scatter_dimension=0, tiled=True)
        all_solved = lax.all_gather(solved, "doc", axis=0, tiled=True)
        lifted = lax.dot_general(features, all_solved, (((0,), (0,)), ((), ())), precision=HI)
        old_weights = weights
        old_margins = margins
        weights = shrink_values(weights + lifted / num_doc, shrink_level / (rho * num_doc))
        margins = logistic_prox(sums + duals_y, signs, weight / rho)
        duals_y = duals_y + sums - margins
        if step + 1 < ITERS:
            move = old_weights - weights
            if step == 0:
                d_move, d_solved, d_applied, d_lifted = (move, solved, applied, lifted)
            else:
                d_move = move - last_move / growth
                d_solved = solved - last_solved / growth
                d_applied = applied - last_applied / growth
                d_lifted = lifted - last_lifted / growth
            primal = (
                jnp.sum(num_doc * d_move * d_move + 2.0 * d_move * d_lifted)
                + jnp.sum(d_solved * d_applied)
                + jnp.sum((sums - margins) ** 2)
            )
            dual = num_doc * jnp.sum(move**2) + jnp.sum((margins - old_margins) ** 2)
            primal, dual = lax.psum((primal, dual), ("doc", "feat"))
            primal = jnp.maximum(primal, 0.0)
            new_product = jnp.dot(features, weights, precision=HI)
            new_product = lax.psum_scatter(new_product, "doc", scatter_dimension=0, tiled=True)
            growth = ((primal + ratio_floor) / (rho * rho * dual + ratio_floor)) ** 0.25
            rho = rho * growth
            duals_y = duals_y / growth
            image = new_product - (product - new_product + applied) / growth
            product = new_product
            last_move, last_solved, last_applied, last_lifted = (move, solved, applied, lifted)
    margins = lax.all_gather(margins, "feat", axis=0, tiled=True)
    weights = lax.all_gather(num_feat * weights, "doc", axis=0, tiled=True)
    return (margins, weights)


def solution(mesh):
    in_specs = (P("doc", "feat"), P("doc", "feat"), P("feat"), P("feat"), P("doc"), P("doc"))
    out_specs = (P("doc", None), P("feat", None))
    return jax.shard_map(
        per_device, mesh=mesh, in_specs=in_specs, out_specs=out_specs, check_vma=False
    )
```

profile of v0, /device:TPU:0, one launch (start us, length us, event | category | flops | bytes accessed | tf_op | source)
XLA Modules:
  0.0 383.9 jit_solution(2985545460666034803)
XLA Ops:
  7.2 2.3 copy.10
  9.4 6.3 %all-to-all-start = ((bf16[128,4,1024]{0,2,1:T(8,128)(2,1)}), bf16[128,4,1024]{0,2,1:T(8,128)(2,1)S(1)}, u32[]{:S(2)}, u32[]{:S(2)}) async-start(bf16[128,4,1024]{0,2,1:T(8,128)(2,1)} %bitcast), calls=%async_computation | async-start | bytes 2097152 | tf_op jit(solution)/shard_map/all_to_all | solution.py:36
  15.8 9.2 %all_gather.31 = bf16[128,512]{0,1:T(8,128)(2,1)S(1)} all-gather(bf16[128,64]{0,1:T(8,128)(2,1)S(1)} %copy-done.4), channel_id=1, replica_groups=mesh['doc'=4,'feat'=8] {'feat'}, dimensions={1}, use_global_device_ids=true | all-gather | bytes 147456 | tf_op jit(solution)/shard_map/all_gather | solution.py:34
  25.0 0.7 dynamic-slice_multiply_fusion
  25.7 25.3 %all_gather.32 = bf16[512,512]{0,1:T(8,128)(2,1)} all-gather(bf16[128,512]{0,1:T(8,128)(2,1)S(1)} %all_gather.31), channel_id=1, replica_groups=mesh['doc'=4,'feat'=8] {'doc'}, dimensions={0}, use_global_device_ids=true | all-gather | bytes 655360 | tf_op jit(solution)/shard_map/all_gather | solution.py:35
  51.0 0.5 copy.11
  51.6 8.3 %cosine_multiply_fusion = f32[512,1024]{1,0:T(8,128)S(1)} fusion(bf16[512,512]{0,1:T(8,128)(2,1)} %all_gather.32, bf16[512,1024]{1,0:T(8,128)(2,1)S(1)} %bitcast.38, f32[1024]{0:T(1024)S(1)} %dynamic-slice-done, f32[1024]{0:T(1024)S(1)} %dynamic-slice_multiply_fusion), kind=kOutput, calls=%fused_computation | convolution fusion | flops 537919488 | bytes 3678208 | tf_op jit(solution)/shard_map/dot_general | solution.py:39
  59.9 2.8 fusion.142
  62.7 0.0 reduce-scatter.7.cloned.1.call-update
  62.7 0.0 reduce-scatter.9.cloned.1.call-start
  62.8 0.1 dynamic-slice
  62.9 0.1 dynamic_slice.12
  62.9 0.1 broadcast_multiply_fusion
  63.1 9.4 %all_gather.30 = f32[128,128]{1,0:T(8,128)S(1)} all-gather(f32[16,128]{1,0:T(8,128)S(1)} %broadcast_multiply_fusion), channel_id=1, replica_groups=mesh['doc'=4,'feat'=8] {'feat'}, dimensions={0}, use_global_device_ids=true | all-gather | bytes 73728 | tf_op jit(solution)/shard_map/all_gather | solution.py:65
  72.5 14.2 %reduce-scatter.7.cloned.1.call-done = f32[1,128,128]{2,1,0:T(8,128)} async-done(((f32[4,128,128]{2,1,0:T(8,128)}), f32[1,128,128]{2,1,0:T(8,128)}) %reduce-scatter.7.cloned.1.call-update) | async-done | bytes 65552 | tf_op jit(solution)/shard_map/reduce_scatter | solution.py:43
  86.7 0.9 bitcast_add_fusion.1
  87.5 0.1 copy.12
  87.6 0.9 fusion.13
  88.5 11.7 %cholesky.18 = f32[128,128]{1,0:T(8,128)S(1)} custom-call(f32[128,128]{1,0:T(8,128)S(1)} %fusion.13), custom_call_target="Cholesky" | custom-call | tf_op jit(solution)/shard_map/jit(cholesky)/cholesky | solution.py:45
  100.2 0.6 compare_reduce_fusion
  100.9 0.7 fusion.10
  101.6 9.8 %custom-call.6 = f32[1,128,128]{1,2,0:T(8,128)S(1)} custom-call(f32[1,128,128]{2,1,0:T(8,128)S(1)} %fusion.10), custom_call_target="InvertDiagBlocksLowerTriangular" | custom-call | tf_op jit(solution)/shard_map/triangular_solve | solution.py:46
  111.4 0.3 fusion.11
  111.6 0.3 fusion.143
  111.9 1.5 multiply_reduce_fusion.3
  113.4 0.0 reduce-scatter.9.cloned.1.call-update
  113.5 0.0 reduce-scatter.11.cloned.1.call-start
  113.5 14.1 %all_gather.33 = f32[512,128]{1,0:T(8,128)S(1)} all-gather(f32[128,128]{1,0:T(8,128)S(1)} %get-tuple-element.23), channel_id=1, replica_groups=mesh['doc'=4,'feat'=8] {'doc'}, dimensions={0}, use_global_device_ids=true | all-gather | bytes 327680 | tf_op jit(solution)/shard_map/all_gather | solution.py:72
  127.6 4.1 %multiply_reduce_fusion.1 = (f32[]{:T(128)}, f32[]{:T(128)}, f32[1024,128]{1,0:T(8,128)S(1)}) fusion(f32[512,1024]{1,0:T(8,128)S(1)} %cosine_multiply_fusion, f32[512,128]{1,0:T(8,128)S(1)} %all_gather.33), kind=kOutput, calls=%fused_computation.13 | convolution fusion | flops 806879232 | bytes 2883592 | tf_op jit(solution)/shard_map/dot_general | solution.py:73
  131.7 2.5 fusion.6
  136.1 0.0 reduce-scatter.11.cloned.1.call-update
  136.1 0.0 reduce-scatter.13.cloned.1.call-start
  136.2 9.2 %reduce-scatter.9.cloned.1.call-done = f32[16,128]{1,0:T(8,128)} async-done(((f32[128,128]{1,0:T(8,128)}), f32[16,128]{1,0:T(8,128)}) %reduce-scatter.9.cloned.1.call-update) | async-done | bytes 8208 | tf_op jit(solution)/shard_map/reduce_scatter | solution.py:71
  145.4 1.5 multiply_reduce_fusion.6
  146.8 1.3 multiply_reduce_fusion.7
  149.3 39.3 %all-reduce.1 = (f32[]{:T(128)}, f32[]{:T(128)}) all-reduce(f32[]{:T(128)S(6)} %add.203, f32[]{:T(128)S(6)} %add.205), channel_id=1, replica_groups=mesh['doc'=4,'feat'=8] {'doc','feat'}, use_global_device_ids=true, to_apply=%region_7.8 | all-reduce | flops 2 | bytes 16 | tf_op jit(solution)/shard_map/psum | solution.py:94
  189.9 0.7 subtract_multiply_fusion.2
  190.6 10.2 %all_gather.34 = f32[128,128]{1,0:T(8,128)S(1)} all-gather(f32[16,128]{1,0:T(8,128)S(1)} %subtract_multiply_fusion.2), channel_id=1, replica_groups=mesh['doc'=4,'feat'=8] {'feat'}, dimensions={0}, use_global_device_ids=true | all-gather | bytes 73728 | tf_op jit(solution)/shard_map/all_gather | solution.py:65
  200.8 0.9 subtract_subtract_fusion
  201.7 1.5 multiply_reduce_fusion.2
  203.2 0.0 reduce-scatter.13.cloned.1.call-update
  203.2 0.0 reduce-scatter.15.cloned.1.call-start
  203.2 14.2 %all_gather.35 = f32[512,128]{1,0:T(8,128)S(1)} all-gather(f32[128,128]{1,0:T(8,128)S(1)} %get-tuple-element.25), channel_id=1, replica_groups=mesh['doc'=4,'feat'=8] {'doc'}, dimensions={0}, use_global_device_ids=true | all-gather | bytes 327680 | tf_op jit(solution)/shard_map/all_gather | solution.py:72
  217.4 4.2 %multiply_reduce_fusion = (f32[]{:T(128)}, f32[]{:T(128)}, f32[1024,128]{1,0:T(8,128)S(1)}) fusion(f32[1024,128]{1,0:T(8,128)S(1)} %get-tuple-element.24, f32[]{:T(128)S(6)} %neg.66, f32[]{:T(128)S(6)} %div.199, f32[]{:T(128)S(6)} %pow.6, f32[512,1024]{1,0:T(8,128)S(1)} %cosine_multiply_fusion, f32[512,128]{1,0:T(8,128)S(1)} %all_gather.35), kind=kOutput, calls=%fused_computation.11 | convolution fusion | flops 808189952 | bytes 3407892 | tf_op jit(solution)/shard_map/dot_general | solution.py:73
  221.6 2.5 fusion.137
  224.1 0.0 reduce-scatter.15.cloned.1.call-update
  224.2 0.0 reduce-scatter.17.cloned.1.call-start
  224.2 0.1 broadcast_divide_fusion.2
  226.1 9.7 %reduce-scatter.13.cloned.1.call-done = f32[16,128]{1,0:T(8,128)} async-done(((f32[128,128]{1,0:T(8,128)}), f32[16,128]{1,0:T(8,128)}) %reduce-scatter.13.cloned.1.call-update) | async-done | bytes 8208 | tf_op jit(solution)/shard_map/reduce_scatter | solution.py:71
  235.9 1.5 multiply_reduce_fusion.4
  238.5 39.4 %all-reduce = (f32[]{:T(128)}, f32[]{:T(128)}) all-reduce(f32[]{:T(128)S(6)} %add.219, f32[]{:T(128)S(6)} %add.221), channel_id=1, replica_groups=mesh['doc'=4,'feat'=8] {'doc','feat'}, use_global_device_ids=true, to_apply=%region_16.17 | all-reduce | flops 2 | bytes 16 | tf_op jit(solution)/shard_map/psum | solution.py:94
  279.2 0.7 subtract_multiply_fusion.1
  279.9 11.2 %all_gather.36 = f32[128,128]{1,0:T(8,128)} all-gather(f32[16,128]{1,0:T(8,128)S(1)} %subtract_multiply_fusion.1), channel_id=1, replica_groups=mesh['doc'=4,'feat'=8] {'feat'}, dimensions={0}, use_global_device_ids=true | all-gather | bytes 73728 | tf_op jit(solution)/shard_map/all_gather | solution.py:65
  291.1 1.8 fusion.140
  292.9 0.0 all-gather.2.cloned.1.call-start
  292.9 14.0 %all_gather.38 = f32[512,128]{1,0:T(8,128)S(1)} all-gather(f32[128,128]{1,0:T(8,128)S(1)} %get-tuple-element.28), channel_id=1, replica_groups=mesh['doc'=4,'feat'=8] {'doc'}, dimensions={0}, use_global_device_ids=true | all-gather | bytes 327680 | tf_op jit(solution)/shard_map/all_gather | solution.py:72
  306.9 4.2 %subtract_multiply_fusion = f32[1024,128]{1,0:T(8,128)} fusion(f32[512,1024]{1,0:T(8,128)S(1)} %cosine_multiply_fusion, f32[512,128]{1,0:T(8,128)S(1)} %all_gather.38, f32[]{:T(128)S(6)} %neg.70, f32[]{:T(128)S(6)} %div.220, f32[]{:T(128)S(6)} %neg.66, f32[]{:T(128)S(6)} %div.199, f32[1024,128]{1,0:T(8,128)S(1)} %get-tuple-element.26, ...), kind=kOutput, calls=%fused_computation.10 | convolution fusion | flops 807141376 | bytes 3932176 | tf_op jit(solution)/shard_map/dot_general | solution.py:73
  311.2 0.1 broadcast_divide_fusion.1
  311.2 14.3 %reduce-scatter.17.cloned.1.call-done = f32[16,128]{1,0:T(8,128)} async-done(((f32[128,128]{1,0:T(8,128)}), f32[16,128]{1,0:T(8,128)}) %reduce-scatter.17.cloned.1.call-update) | async-done | bytes 8208 | tf_op jit(solution)/shard_map/reduce_scatter | solution.py:71
  325.6 0.8 fusion.63
  326.4 9.2 %all_gather.37 = f32[128,128]{1,0:T(8,128)S(1)} all-gather(f32[16,128]{1,0:T(8,128)S(1)} %fusion.63), channel_id=1, replica_groups=mesh['doc'=4,'feat'=8] {'feat'}, dimensions={0}, use_global_device_ids=true | all-gather | bytes 73728 | tf_op jit(solution)/shard_map/all_gather | solution.py:104
  335.6 37.8 %all-gather.2.cloned.1.call-done = f32[4096,128]{1,0:T(8,128)} async-done(((f32[1024,128]{1,0:T(8,128)}), f32[4096,128]{1,0:T(8,128)}) %all-gather.2.cloned.1.call-update) | async-done | bytes 2097168 | tf_op jit(solution)/shard_map/all_gather | solution.py:105
  373.4 0.6 copy.15
  374.0 3.0 copy.16
  (29 shorter events, 0.1 us)
Async XLA Ops:
  7.2 8.6 %copy-start.4 = (bf16[128,64]{0,1:T(8,128)(2,1)S(1)}, bf16[128,64]{0,1:T(8,128)(2,1)}, u32[]{:S(2)}) copy-start(bf16[128,64]{0,1:T(8,128)(2,1)} %param.6) | copy-start | bytes 49156
  9.4 41.6 %all-to-all-start = ((bf16[128,4,1024]{0,2,1:T(8,128)(2,1)}), bf16[128,4,1024]{0,2,1:T(8,128)(2,1)S(1)}, u32[]{:S(2)}, u32[]{:S(2)}) async-start(bf16[128,4,1024]{0,2,1:T(8,128)(2,1)} %bitcast), calls=%async_computation | async-start | bytes 2097152 | tf_op jit(solution)/shard_map/all_to_all | solution.py:36
  15.8 70.9 %reduce-scatter.7.cloned.1.call-start = ((), (), s32[]{:S(2)}) async-start(), calls=%async_computation.7 | async-start | bytes 327680 | tf_op jit(solution)/shard_map/reduce_scatter | solution.py:43
  15.8 35.8 %dynamic-slice-start = ((f32[4096]{0:T(1024)}, s32[]{:T(128)}), f32[1024]{0:T(1024)S(1)}, s32[]{:S(2)}) async-start(f32[4096]{0:T(1024)} %param.8, s32[]{:T(128)} %select_n.18), calls=%async_computation.14 | async-start | bytes 8704 | tf_op jit(solution)/shard_map/dynamic_slice | solution.py:37
  59.9 2.9 copy-start.9
  59.9 2.9 copy-start.7
  62.7 82.6 %reduce-scatter.9.cloned.1.call-start = ((), (), s32[]{:S(2)}) async-start(), calls=%async_computation.8 | async-start | bytes 73728 | tf_op jit(solution)/shard_map/reduce_scatter | solution.py:71
  62.9 173.0 %copy-start.5 = (s32[16]{0:T(128)}, s32[16]{0:T(128)S(1)}, u32[]{:S(2)}) copy-start(s32[16]{0:T(128)S(1)} %dynamic-slice) | copy-start | bytes 196
  113.5 87.4 %reduce-scatter.11.cloned.1.call-start = ((), (), s32[]{:S(2)}) async-start(), calls=%async_computation.9 | async-start | bytes 327680 | tf_op jit(solution)/shard_map/reduce_scatter | solution.py:97
  131.7 69.2 %copy-start = (f32[128,128]{1,0:T(8,128)S(1)}, f32[128,128]{1,0:T(8,128)}, u32[]{:S(2)}) copy-start(f32[128,128]{1,0:T(8,128)} %get-tuple-element.20) | copy-start | bytes 196612
  136.1 99.8 %reduce-scatter.13.cloned.1.call-start = ((), (), s32[]{:S(2)}) async-start(), calls=%async_computation.10 | async-start | bytes 73728 | tf_op jit(solution)/shard_map/reduce_scatter | solution.py:71
  203.2 87.9 %reduce-scatter.15.cloned.1.call-start = ((), (), s32[]{:S(2)}) async-start(), calls=%async_computation.11 | async-start | bytes 327680 | tf_op jit(solution)/shard_map/reduce_scatter | solution.py:97
  221.6 69.5 %copy-start.1 = (f32[128,128]{1,0:T(8,128)S(1)}, f32[128,128]{1,0:T(8,128)}, u32[]{:S(2)}) copy-start(f32[128,128]{1,0:T(8,128)} %reduce-scatter.11.cloned.1.call-done) | copy-start | bytes 196612
  221.6 69.5 %copy-start.2 = (f32[128,128]{1,0:T(8,128)S(1)}, f32[128,128]{1,0:T(8,128)}, u32[]{:S(2)}) copy-start(f32[128,128]{1,0:T(8,128)} %get-tuple-element.22) | copy-start | bytes 196612
  224.2 101.4 %reduce-scatter.17.cloned.1.call-start = ((), (), s32[]{:S(2)}) async-start(), calls=%async_computation.12 | async-start | bytes 73728 | tf_op jit(solution)/shard_map/reduce_scatter | solution.py:71
  292.9 80.5 %all-gather.2.cloned.1.call-start = ((), (), s32[]{:S(2)}) async-start(), calls=%async_computation.13 | async-start | bytes 2621440 | tf_op jit(solution)/shard_map/all_gather | solution.py:105
  306.9 4.3 %copy-start.8 = (f32[128]{0:T(128)S(1)}, f32[128]{0:T(128)}, u32[]{:S(2)}) copy-start(f32[128]{0:T(128)} %param.10) | copy-start | bytes 1540
  306.9 18.7 %copy-start.3 = (f32[16,128]{1,0:T(8,128)S(1)}, f32[16,128]{1,0:T(8,128)}, u32[]{:S(2)}) copy-start(f32[16,128]{1,0:T(8,128)} %reduce-scatter.13.cloned.1.call-done) | copy-start | bytes 24580
  306.9 18.7 %copy-start.6 = (s32[16]{0:T(128)S(1)}, s32[16]{0:T(128)}, u32[]{:S(2)}) copy-start(s32[16]{0:T(128)} %copy-done.5) | copy-start | bytes 196
Sparse Core Ops, SparseCore 0:
  62.8 23.8 reduce-scatter.6
  113.6 31.7 reduce-scatter.8
  148.2 19.9 reduce-scatter.10
  203.3 32.4 reduce-scatter.12
  238.5 19.9 reduce-scatter.14
  293.0 32.5 reduce-scatter.16
  327.7 45.6 all-gather.1
where the time goes:
time: 385 us; the launch traced here: 384 us
  blocking collectives  195 us (51%)
  waiting for transfers between devices  85.3 us (22%)
  matrix products  33.9 us (9%)
  other arithmetic  32.9 us (9%)
  between operations  23 us (6%)
  local copies, waits for them, and re-layouts  6.75 us (2%)
  starting transfers between devices  6.6 us (2%)
    psum x2, blocking collectives, per_device(): primal, dual = lax.psum((primal, dual), ('doc', 'feat'))  78.7 us
    all_gather x3, blocking collectives, per_device(): all_solved = lax.all_gather(solved, 'doc', axis=0, tiled=True)  42.2 us
    all_gather x1, waiting for transfers between devices, per_device(): weights = lax.all_gather(num_feat * weights, 'doc', axis=0, tiled=True)  37.8 us
    reduce_scatter x3, waiting for transfers between devices, per_device(): sums = lax.psum_scatter(part, 'feat', scatter_dimension=0, tiled=True)  33.2 us
    all_gather x3, blocking collectives, per_device(): correction = lax.all_gather(correction, 'feat', axis=0, tiled=True)  30.8 us
    all_gather x1, blocking collectives, per_device(): doc_full = lax.all_gather(doc_rows, 'doc', axis=0, tiled=True)  25.3 us
    reduce_scatter x1, waiting for transfers between devices, per_device(): gram = lax.psum_scatter(gram, 'doc', scatter_dimension=0, tiled=True)[0]  14.2 us
    dot_general x3, matrix products, per_device(): lax.dot_general(features, all_solved, (((0,), (0,)), ((), ())), precision...  12.5 us
  transfers between devices with their start and end apart: 8, of which 5 were waited for; matrix products, arithmetic and copies ran while one was open for 7% of the time, Pallas kernels for 0%

commit v1 on v0

--- a/solution.py
+++ b/solution.py
@@ -9,6 +9,18 @@
 HI = lax.Precision.HIGHEST
 shrink_level = 0.1
 ratio_floor = 1e-06
+
+
+def gather_by_bits(x, axis, dim):
+    ways, here = (lax.axis_size(axis), lax.axis_index(axis))
+    grown, reach = (x, 1)
+    while reach < ways:
+        theirs = lax.ppermute(grown, axis, [(d, d ^ reach) for d in range(ways)])
+        mine_first = jnp.concatenate([grown, theirs], axis=dim)
+        theirs_first = jnp.concatenate([theirs, grown], axis=dim)
+        grown = jnp.where(here & reach == 0, mine_first, theirs_first)
+        reach = 2 * reach
+    return grown
 
 
 def logistic_prox(target, signs, weight_ratio):
@@ -69,7 +81,7 @@
         applied = residue - solved
         part = target - solved
         sums = lax.psum_scatter(part, "feat", scatter_dimension=0, tiled=True)
-        all_solved = lax.all_gather(solved, "doc", axis=0, tiled=True)
+        all_solved = gather_by_bits(solved, "doc", 0)
         lifted = lax.dot_general(features, all_solved, (((0,), (0,)), ((), ())), precision=HI)
         old_weights = weights
         old_margins = margins

time: 385 us -> 406 us (1.055)
  waiting for transfers between devices: 85.3 us -> 140 us
  blocking collectives: 195 us -> 152 us
  starting transfers between devices: 6.6 us -> 15.8 us
    all_gather x3 -> x0, blocking collectives: 42.2 us -> none  [per_device(): all_solved = lax.all_gather(solved, 'doc', axis=0, tiled=True)]
    ppermute x0 -> x6, waiting for transfers between devices: none -> 28.2 us  [gather_by_bits(): theirs = lax.ppermute(grown, axis, [(d, d ^ reach) for d in range(ways)])]
    reduce_scatter x3, waiting for transfers between devices: 33.2 us -> 59.4 us  [per_device(): sums = lax.psum_scatter(part, 'feat', scatter_dimension=0, tiled=True)]
    ppermute x0 -> x6, starting transfers between devices: none -> 8.7 us  [gather_by_bits(): theirs = lax.ppermute(grown, axis, [(d, d ^ reach) for d in range(ways)])]
  transfers between devices with their start and end apart: 8 -> 14, of which waited for: 5 -> 11; matrix products, arithmetic and copies ran while one was open for 7% -> 6% of each run, Pallas kernels for 0% -> 0%
where the time goes in v1:
time: 406 us; the launch traced here: 405 us
  blocking collectives  152 us (37%)
  waiting for transfers between devices  140 us (34%)
  matrix products  34.7 us (9%)
  other arithmetic  33 us (8%)
  between operations  23.2 us (6%)
  starting transfers between devices  15.8 us (4%)
  local copies, waits for them, and re-layouts  6.76 us (2%)
    psum x2, blocking collectives, per_device(): primal, dual = lax.psum((primal, dual), ('doc', 'feat'))  78.6 us
    reduce_scatter x3, waiting for transfers between devices, per_device(): sums = lax.psum_scatter(part, 'feat', scatter_dimension=0, tiled=True)  59.4 us
    all_gather x1, waiting for transfers between devices, per_device(): weights = lax.all_gather(num_feat * weights, 'doc', axis=0, tiled=True)  37.8 us
    all_gather x3, blocking collectives, per_device(): correction = lax.all_gather(correction, 'feat', axis=0, tiled=True)  29.9 us
    ppermute x6, waiting for transfers between devices, gather_by_bits(): theirs = lax.ppermute(grown, axis, [(d, d ^ reach) for d in range(ways)])  28.2 us
    all_gather x1, blocking collectives, per_device(): doc_full = lax.all_gather(doc_rows, 'doc', axis=0, tiled=True)  25.3 us
    reduce_scatter x1, waiting for transfers between devices, per_device(): gram = lax.psum_scatter(gram, 'doc', scatter_dimension=0, tiled=True)[0]  14.2 us
    dot_general x3, matrix products, per_device(): lax.dot_general(features, all_solved, (((0,), (0,)), ((), ())), precision...  13.5 us
  transfers between devices with their start and end apart: 14, of which 11 were waited for; matrix products, arithmetic and copies ran while one was open for 6% of the time, Pallas kernels for 0%

profile of v1, /device:TPU:0, one launch (start us, length us, event | category | flops | bytes accessed | tf_op | source)
XLA Modules:
  0.0 405.3 jit_solution(5055399684375657936)
XLA Ops:
  7.2 2.3 copy.10
  9.4 6.3 %all-to-all-start = ((bf16[128,4,1024]{0,2,1:T(8,128)(2,1)}), bf16[128,4,1024]{0,2,1:T(8,128)(2,1)S(1)}, u32[]{:S(2)}, u32[]{:S(2)}) async-start(bf16[128,4,1024]{0,2,1:T(8,128)(2,1)} %bitcast), calls=%async_computation | async-start | bytes 2097152 | tf_op jit(solution)/shard_map/all_to_all | solution.py:48
  15.8 9.2 %all_gather.22 = bf16[128,512]{0,1:T(8,128)(2,1)S(1)} all-gather(bf16[128,64]{0,1:T(8,128)(2,1)S(1)} %copy-done.6), channel_id=1, replica_groups=mesh['doc'=4,'feat'=8] {'feat'}, dimensions={1}, use_global_device_ids=true | all-gather | bytes 147456 | tf_op jit(solution)/shard_map/all_gather | solution.py:46
  25.0 0.7 dynamic-slice_multiply_fusion
  25.7 25.3 %all_gather.23 = bf16[512,512]{0,1:T(8,128)(2,1)} all-gather(bf16[128,512]{0,1:T(8,128)(2,1)S(1)} %all_gather.22), channel_id=1, replica_groups=mesh['doc'=4,'feat'=8] {'doc'}, dimensions={0}, use_global_device_ids=true | all-gather | bytes 655360 | tf_op jit(solution)/shard_map/all_gather | solution.py:47
  51.0 0.5 copy.11
  51.6 8.3 %cosine_multiply_fusion = f32[512,1024]{1,0:T(8,128)S(1)} fusion(bf16[512,512]{0,1:T(8,128)(2,1)} %all_gather.23, bf16[512,1024]{1,0:T(8,128)(2,1)S(1)} %bitcast.35, f32[1024]{0:T(1024)S(1)} %dynamic-slice-done, f32[1024]{0:T(1024)S(1)} %dynamic-slice_multiply_fusion), kind=kOutput, calls=%fused_computation | convolution fusion | flops 537919488 | bytes 3678208 | tf_op jit(solution)/shard_map/dot_general | solution.py:51
  59.9 2.8 fusion.165
  62.8 0.1 dynamic-slice
  62.9 0.1 dynamic_slice.12
  62.9 0.1 broadcast_multiply_fusion
  63.1 9.4 %all_gather.21 = f32[128,128]{1,0:T(8,128)S(1)} all-gather(f32[16,128]{1,0:T(8,128)S(1)} %broadcast_multiply_fusion), channel_id=1, replica_groups=mesh['doc'=4,'feat'=8] {'feat'}, dimensions={0}, use_global_device_ids=true | all-gather | bytes 73728 | tf_op jit(solution)/shard_map/all_gather | solution.py:77
  72.5 14.2 %reduce-scatter.7.cloned.1.call-done = f32[1,128,128]{2,1,0:T(8,128)} async-done(((f32[4,128,128]{2,1,0:T(8,128)}), f32[1,128,128]{2,1,0:T(8,128)}) %reduce-scatter.7.cloned.1.call-update) | async-done | bytes 65552 | tf_op jit(solution)/shard_map/reduce_scatter | solution.py:55
  86.7 0.9 bitcast_add_fusion.1
  87.5 0.1 copy.12
  87.6 0.9 fusion.33
  88.5 11.7 %cholesky.18 = f32[128,128]{1,0:T(8,128)S(1)} custom-call(f32[128,128]{1,0:T(8,128)S(1)} %fusion.33), custom_call_target="Cholesky" | custom-call | tf_op jit(solution)/shard_map/jit(cholesky)/cholesky | solution.py:57
  100.2 0.6 compare_reduce_fusion
  100.9 0.7 fusion.30
  101.6 9.8 %custom-call.6 = f32[1,128,128]{1,2,0:T(8,128)S(1)} custom-call(f32[1,128,128]{2,1,0:T(8,128)S(1)} %fusion.30), custom_call_target="InvertDiagBlocksLowerTriangular" | custom-call | tf_op jit(solution)/shard_map/triangular_solve | solution.py:58
  111.4 0.2 fusion.31
  111.6 0.3 fusion.166
  111.9 1.4 multiply_reduce_fusion.3
  113.3 4.4 %collective-permute-done = f32[128,128]{1,0:T(8,128)S(1)} collective-permute-done((f32[128,128]{1,0:T(8,128)S(1)}, f32[128,128]{1,0:T(8,128)S(1)}, u32[]{:S(2)}, u32[]{:S(2)}) %collective-permute-start) | collective-permute-done | bytes 65568 | tf_op jit(solution)/shard_map/ppermute | solution.py:18
  117.8 1.1 collective-permute-start.1
  118.9 0.3 reduce-scatter.11.cloned.1.call-start
  119.2 5.6 %collective-permute-done.1 = f32[256,128]{1,0:T(8,128)S(1)} collective-permute-done((f32[256,128]{1,0:T(8,128)S(1)}, f32[256,128]{1,0:T(8,128)S(1)}, u32[]{:S(2)}, u32[]{:S(2)}) %collective-permute-start.1) | collective-permute-done | bytes 131104 | tf_op jit(solution)/shard_map/ppermute | solution.py:18
  124.8 4.1 %multiply_reduce_fusion.1 = (f32[]{:T(128)}, f32[]{:T(128)}, f32[1024,128]{1,0:T(8,128)S(1)}) fusion(f32[512,1024]{1,0:T(8,128)S(1)} %cosine_multiply_fusion, f32[256,128]{1,0:T(8,128)S(1)} %collective-permute-done.1, f32[256,128]{1,0:T(8,128)S(1)} %maximum_select_fusion.6, pred[]{:T(512)S(6)} %eq.13), kind=kOutput, calls=%fused_computation.13 | convolution fusion | flops 807075840 | bytes 2883593 | tf_op jit(solution)/shard_map/dot_general | solution.py:85
  128.9 2.5 fusion.6
  131.5 20.5 %reduce-scatter.9.cloned.1.call-done = f32[16,128]{1,0:T(8,128)} async-done(((f32[128,128]{1,0:T(8,128)}), f32[16,128]{1,0:T(8,128)}) %reduce-scatter.9.cloned.1.call-update) | async-done | bytes 8208 | tf_op jit(solution)/shard_map/reduce_scatter | solution.py:83
  152.0 1.5 multiply_reduce_fusion.6
  153.5 1.3 multiply_reduce_fusion.7
  157.9 39.3 %all-reduce.1 = (f32[]{:T(128)}, f32[]{:T(128)}) all-reduce(f32[]{:T(128)S(6)} %add.203, f32[]{:T(128)S(6)} %add.205), channel_id=1, replica_groups=mesh['doc'=4,'feat'=8] {'doc','feat'}, use_global_device_ids=true, to_apply=%region_7.8 | all-reduce | flops 2 | bytes 16 | tf_op jit(solution)/shard_map/psum | solution.py:106
  198.5 0.7 subtract_multiply_fusion.2
  199.2 10.2 %all_gather.24 = f32[128,128]{1,0:T(8,128)S(1)} all-gather(f32[16,128]{1,0:T(8,128)S(1)} %subtract_multiply_fusion.2), channel_id=1, replica_groups=mesh['doc'=4,'feat'=8] {'feat'}, dimensions={0}, use_global_device_ids=true | all-gather | bytes 73728 | tf_op jit(solution)/shard_map/all_gather | solution.py:77
  209.4 0.9 subtract_subtract_fusion
  210.3 1.4 multiply_reduce_fusion.2
  211.7 1.5 collective-permute-start.2
  213.2 2.9 collective-permute-done.2
  216.1 2.3 collective-permute-start.3
  218.5 0.3 reduce-scatter.15.cloned.1.call-start
  218.8 6.1 %collective-permute-done.3 = f32[256,128]{1,0:T(8,128)} collective-permute-done((f32[256,128]{1,0:T(8,128)S(1)}, f32[256,128]{1,0:T(8,128)}, u32[]{:S(2)}, u32[]{:S(2)}) %collective-permute-start.3) | collective-permute-done | bytes 131104 | tf_op jit(solution)/shard_map/ppermute | solution.py:18
  224.9 5.2 %multiply_reduce_fusion = (f32[]{:T(128)}, f32[]{:T(128)}, f32[1024,128]{1,0:T(8,128)S(1)}) fusion(f32[1024,128]{1,0:T(8,128)S(1)} %get-tuple-element.24, f32[]{:T(128)S(6)} %neg.66, f32[]{:T(128)S(6)} %div.199, f32[]{:T(128)S(6)} %pow.6, f32[512,1024]{1,0:T(8,128)S(1)} %cosine_multiply_fusion, f32[256,128]{1,0:T(8,128)} %collective-permute-done.3, ...), kind=kOutput, calls=%fused_computation.11 | convolution fusion | flops 808386560 | bytes 3407893 | tf_op jit(solution)/shard_map/dot_general | solution.py:85
  230.1 2.5 fusion.160
  232.6 0.0 reduce-scatter.17.cloned.1.call-start
  232.7 0.1 broadcast_divide_fusion.2
  232.8 17.6 %reduce-scatter.13.cloned.1.call-done = f32[16,128]{1,0:T(8,128)} async-done(((f32[128,128]{1,0:T(8,128)}), f32[16,128]{1,0:T(8,128)}) %reduce-scatter.13.cloned.1.call-update) | async-done | bytes 8208 | tf_op jit(solution)/shard_map/reduce_scatter | solution.py:83
  250.4 1.5 multiply_reduce_fusion.4
  255.0 39.3 %all-reduce = (f32[]{:T(128)}, f32[]{:T(128)}) all-reduce(f32[]{:T(128)S(6)} %add.219, f32[]{:T(128)S(6)} %add.221), channel_id=1, replica_groups=mesh['doc'=4,'feat'=8] {'doc','feat'}, use_global_device_ids=true, to_apply=%region_16.17 | all-reduce | flops 2 | bytes 16 | tf_op jit(solution)/shard_map/psum | solution.py:106
  295.6 0.7 subtract_multiply_fusion.1
  296.3 10.2 %all_gather.25 = f32[128,128]{1,0:T(8,128)S(1)} all-gather(f32[16,128]{1,0:T(8,128)S(1)} %subtract_multiply_fusion.1), channel_id=1, replica_groups=mesh['doc'=4,'feat'=8] {'feat'}, dimensions={0}, use_global_device_ids=true | all-gather | bytes 73728 | tf_op jit(solution)/shard_map/all_gather | solution.py:77
  306.6 1.7 fusion.163
  308.2 1.5 collective-permute-start.4
  309.7 2.9 collective-permute-done.4
  312.6 2.3 collective-permute-start.5
  315.2 6.2 %collective-permute-done.5 = f32[256,128]{1,0:T(8,128)S(1)} collective-permute-done((f32[256,128]{1,0:T(8,128)S(1)}, f32[256,128]{1,0:T(8,128)S(1)}, u32[]{:S(2)}, u32[]{:S(2)}) %collective-permute-start.5) | collective-permute-done | bytes 131104 | tf_op jit(solution)/shard_map/ppermute | solution.py:18
  321.3 4.2 %subtract_multiply_fusion = f32[1024,128]{1,0:T(8,128)} fusion(f32[512,1024]{1,0:T(8,128)S(1)} %cosine_multiply_fusion, f32[256,128]{1,0:T(8,128)S(1)} %collective-permute-done.5, f32[256,128]{1,0:T(8,128)S(1)} %maximum_select_fusion.8, f32[]{:T(128)S(6)} %neg.70, f32[]{:T(128)S(6)} %div.220, pred[]{:T(512)S(6)} %eq.13, f32[]{:T(128)S(6)} %neg.66, ...), kind=kOutput, calls=%fused_computation.10 | convolution fusion | flops 807337984 | bytes 3932177 | tf_op jit(solution)/shard_map/dot_general | solution.py:85
  325.6 0.1 broadcast_divide_fusion.1
  325.7 21.2 %reduce-scatter.17.cloned.1.call-done = f32[16,128]{1,0:T(8,128)} async-done(((f32[128,128]{1,0:T(8,128)}), f32[16,128]{1,0:T(8,128)}) %reduce-scatter.17.cloned.1.call-update) | async-done | bytes 8208 | tf_op jit(solution)/shard_map/reduce_scatter | solution.py:83
  346.9 0.8 fusion.83
  347.8 9.2 %all_gather.26 = f32[128,128]{1,0:T(8,128)S(1)} all-gather(f32[16,128]{1,0:T(8,128)S(1)} %fusion.83), channel_id=1, replica_groups=mesh['doc'=4,'feat'=8] {'feat'}, dimensions={0}, use_global_device_ids=true | all-gather | bytes 73728 | tf_op jit(solution)/shard_map/all_gather | solution.py:116
  357.0 37.8 %all-gather.2.cloned.1.call-done = f32[4096,128]{1,0:T(8,128)} async-done(((f32[1024,128]{1,0:T(8,128)}), f32[4096,128]{1,0:T(8,128)}) %all-gather.2.cloned.1.call-update) | async-done | bytes 2097168 | tf_op jit(solution)/shard_map/all_gather | solution.py:117
  394.8 0.6 copy.15
  395.4 3.0 copy.16
  (49 shorter events, 0.4 us)
Async XLA Ops:
  7.2 8.6 %copy-start.6 = (bf16[128,64]{0,1:T(8,128)(2,1)S(1)}, bf16[128,64]{0,1:T(8,128)(2,1)}, u32[]{:S(2)}) copy-start(bf16[128,64]{0,1:T(8,128)(2,1)} %param.6) | copy-start | bytes 49156
  9.4 41.6 %all-to-all-start = ((bf16[128,4,1024]{0,2,1:T(8,128)(2,1)}), bf16[128,4,1024]{0,2,1:T(8,128)(2,1)S(1)}, u32[]{:S(2)}, u32[]{:S(2)}) async-start(bf16[128,4,1024]{0,2,1:T(8,128)(2,1)} %bitcast), calls=%async_computation | async-start | bytes 2097152 | tf_op jit(solution)/shard_map/all_to_all | solution.py:48
  15.8 70.9 %reduce-scatter.7.cloned.1.call-start = ((), (), s32[]{:S(2)}) async-start(), calls=%async_computation.7 | async-start | bytes 327680 | tf_op jit(solution)/shard_map/reduce_scatter | solution.py:55
  15.8 35.8 %dynamic-slice-start = ((f32[4096]{0:T(1024)}, s32[]{:T(128)}), f32[1024]{0:T(1024)S(1)}, s32[]{:S(2)}) async-start(f32[4096]{0:T(1024)} %param.8, s32[]{:T(128)} %select_n.50), calls=%async_computation.14 | async-start | bytes 8704 | tf_op jit(solution)/shard_map/dynamic_slice | solution.py:49
  59.9 2.9 copy-start.13
  59.9 2.9 copy-start.10
  62.7 89.3 %reduce-scatter.9.cloned.1.call-start = ((), (), s32[]{:S(2)}) async-start(), calls=%async_computation.8 | async-start | bytes 73728 | tf_op jit(solution)/shard_map/reduce_scatter | solution.py:83
  62.9 89.2 %copy-start.7 = (s32[16]{0:T(128)}, s32[16]{0:T(128)S(1)}, u32[]{:S(2)}) copy-start(s32[16]{0:T(128)S(1)} %dynamic-slice) | copy-start | bytes 196
  113.3 4.4 %collective-permute-start = (f32[128,128]{1,0:T(8,128)S(1)}, f32[128,128]{1,0:T(8,128)S(1)}, u32[]{:S(2)}, u32[]{:S(2)}) collective-permute-start(f32[128,128]{1,0:T(8,128)S(1)} %get-tuple-element.23), channel_id=1, source_target_pairs={{0,8},{8,0},{16,24},{24,16},{1,9},{9,1},{17,25},{25,17},{2,10},{10... | collective-permute-start | bytes 196616 | tf_op jit(solution)/shard_map/ppermute | solution.py:18
  117.8 7.0 %collective-permute-start.1 = (f32[256,128]{1,0:T(8,128)S(1)}, f32[256,128]{1,0:T(8,128)S(1)}, u32[]{:S(2)}, u32[]{:S(2)}) collective-permute-start(f32[256,128]{1,0:T(8,128)S(1)} %maximum_select_fusion.6), channel_id=1, source_target_pairs={{0,16},{8,24},{16,0},{24,8},{1,17},{9,25},{17,1},{25,9},{2,18},{10... | collective-permute-start | bytes 393224 | tf_op jit(solution)/shard_map/ppermute | solution.py:18
  118.9 90.5 %reduce-scatter.11.cloned.1.call-start = ((), (), s32[]{:S(2)}) async-start(), calls=%async_computation.9 | async-start | bytes 327680 | tf_op jit(solution)/shard_map/reduce_scatter | solution.py:109
  128.9 80.5 %copy-start = (f32[128,128]{1,0:T(8,128)S(1)}, f32[128,128]{1,0:T(8,128)}, u32[]{:S(2)}) copy-start(f32[128,128]{1,0:T(8,128)} %get-tuple-element.20) | copy-start | bytes 196612
  131.4 119.0 %reduce-scatter.13.cloned.1.call-start = ((), (), s32[]{:S(2)}) async-start(), calls=%async_computation.10 | async-start | bytes 73728 | tf_op jit(solution)/shard_map/reduce_scatter | solution.py:83
  211.7 4.4 %collective-permute-start.2 = (f32[128,128]{1,0:T(8,128)S(1)}, f32[128,128]{1,0:T(8,128)S(1)}, u32[]{:S(2)}, u32[]{:S(2)}) collective-permute-start(f32[128,128]{1,0:T(8,128)S(1)} %get-tuple-element.25), channel_id=1, source_target_pairs={{0,8},{8,0},{16,24},{24,16},{1,9},{9,1},{17,25},{25,17},{2,10},{10... | collective-permute-start | bytes 196616 | tf_op jit(solution)/shard_map/ppermute | solution.py:18
  216.1 8.8 %collective-permute-start.3 = (f32[256,128]{1,0:T(8,128)S(1)}, f32[256,128]{1,0:T(8,128)}, u32[]{:S(2)}, u32[]{:S(2)}) collective-permute-start(f32[256,128]{1,0:T(8,128)S(1)} %maximum_select_fusion.7), channel_id=1, source_target_pairs={{0,16},{8,24},{16,0},{24,8},{1,17},{9,25},{17,1},{25,9},{2,18},{10... | collective-permute-start | bytes 393224 | tf_op jit(solution)/shard_map/ppermute | solution.py:18
  218.5 88.0 %reduce-scatter.15.cloned.1.call-start = ((), (), s32[]{:S(2)}) async-start(), calls=%async_computation.11 | async-start | bytes 327680 | tf_op jit(solution)/shard_map/reduce_scatter | solution.py:109
  230.1 2.6 copy-start.11
  230.1 20.3 %copy-start.8 = (s32[16]{0:T(128)S(1)}, s32[16]{0:T(128)}, u32[]{:S(2)}) copy-start(s32[16]{0:T(128)} %copy-done.7) | copy-start | bytes 196
  230.1 76.5 %copy-start.1 = (f32[128,128]{1,0:T(8,128)S(1)}, f32[128,128]{1,0:T(8,128)}, u32[]{:S(2)}) copy-start(f32[128,128]{1,0:T(8,128)} %reduce-scatter.11.cloned.1.call-done) | copy-start | bytes 196612
  230.1 76.5 %copy-start.2 = (f32[128,128]{1,0:T(8,128)S(1)}, f32[128,128]{1,0:T(8,128)}, u32[]{:S(2)}) copy-start(f32[128,128]{1,0:T(8,128)} %get-tuple-element.22) | copy-start | bytes 196612
  232.6 114.3 %reduce-scatter.17.cloned.1.call-start = ((), (), s32[]{:S(2)}) async-start(), calls=%async_computation.12 | async-start | bytes 73728 | tf_op jit(solution)/shard_map/reduce_scatter | solution.py:83
  251.9 43.7 %copy-start.4 = (f32[16,128]{1,0:T(8,128)}, f32[16,128]{1,0:T(8,128)S(1)}, u32[]{:S(2)}) copy-start(f32[16,128]{1,0:T(8,128)S(1)} %get-tuple-element.12) | copy-start | bytes 24580
  308.2 4.4 %collective-permute-start.4 = (f32[128,128]{1,0:T(8,128)S(1)}, f32[128,128]{1,0:T(8,128)S(1)}, u32[]{:S(2)}, u32[]{:S(2)}) collective-permute-start(f32[128,128]{1,0:T(8,128)S(1)} %get-tuple-element.28), channel_id=1, source_target_pairs={{0,8},{8,0},{16,24},{24,16},{1,9},{9,1},{17,25},{25,17},{2,10},{10... | collective-permute-start | bytes 196616 | tf_op jit(solution)/shard_map/ppermute | solution.py:18
  312.6 8.7 %collective-permute-start.5 = (f32[256,128]{1,0:T(8,128)S(1)}, f32[256,128]{1,0:T(8,128)S(1)}, u32[]{:S(2)}, u32[]{:S(2)}) collective-permute-start(f32[256,128]{1,0:T(8,128)S(1)} %maximum_select_fusion.8), channel_id=1, source_target_pairs={{0,16},{8,24},{16,0},{24,8},{1,17},{9,25},{17,1},{25,9},{2,18},{10... | collective-permute-start | bytes 393224 | tf_op jit(solution)/shard_map/ppermute | solution.py:18
  315.1 10.5 %copy-start.12 = (f32[128]{0:T(128)S(1)}, f32[128]{0:T(128)}, u32[]{:S(2)}) copy-start(f32[128]{0:T(128)} %param.10) | copy-start | bytes 1540
  315.1 31.9 %copy-start.3 = (f32[16,128]{1,0:T(8,128)S(1)}, f32[16,128]{1,0:T(8,128)}, u32[]{:S(2)}) copy-start(f32[16,128]{1,0:T(8,128)} %reduce-scatter.13.cloned.1.call-done) | copy-start | bytes 24580
  315.1 31.9 %copy-start.5 = (f32[16,128]{1,0:T(8,128)S(1)}, f32[16,128]{1,0:T(8,128)}, u32[]{:S(2)}) copy-start(f32[16,128]{1,0:T(8,128)} %copy-done.4) | copy-start | bytes 24580
  315.1 31.9 %copy-start.9 = (s32[16]{0:T(128)S(1)}, s32[16]{0:T(128)}, u32[]{:S(2)}) copy-start(s32[16]{0:T(128)} %copy-done.7) | copy-start | bytes 196
  315.1 79.7 %all-gather.2.cloned.1.call-start = ((), (), s32[]{:S(2)}) async-start(), calls=%async_computation.13 | async-start | bytes 2621440 | tf_op jit(solution)/shard_map/all_gather | solution.py:117
Sparse Core Ops, SparseCore 0:
  62.8 23.8 reduce-scatter.6
  119.0 32.9 reduce-scatter.8
  154.9 19.9 reduce-scatter.10
  218.6 31.7 reduce-scatter.12
  253.1 19.9 reduce-scatter.14
  315.2 31.7 reduce-scatter.16
  349.1 45.6 all-gather.1
